TPU v7x, 512 devices: a whole 4x8x8 slice. The times are simulated.
512 devices in a mesh: tm: 64 (over y, z_lo, core), sta: 8 (over x, z_hi).
Axes of the slice: x: 4, y: 8, z: 8 (z_hi: 2, z_lo: 4; z = z_hi * 4 + z_lo), core: 2. Of those that a mesh axis runs over, the one named last changes fastest.
Arguments:
- data: bfloat16 [64, 3, 24576], P('sta', None, 'tm'), as said below
- bank: bfloat16 [64, 8, 64, 3, 150], P('tm', None, 'sta'), may hold values from -6 to 6
- owners: int32 [2], replicated, may hold values from 0 to 63
- moveouts: int32 [2, 8, 64], P(None, None, 'sta'), may hold values from 0 to 64, as said below
Outputs:
- stack: float32 [2, 8, 24576], P(None, 'sta', 'tm')
Inputs may be any that keep to these rules, and one draw needn't show every extreme that they name: `data`: three-component records with amplitudes that vary from station to station and along time. `moveouts`: delays are relative to the earliest arrival: for each template some station has 0 and some other station has 64.
All inputs are finite; a program needn't handle non-finite values.
Results may differ from a plain program's by a relative error of at most 0.0003.
Values may be sent and summed in bfloat16 or wider, within the bound.
No kernel may reach another device: no remote copies, remote signals or barrier semaphores. Data moves between devices by JAX's collectives and lax.ppermute only.
A program may use at most 64 MiB of HBM per device.

v0:
```python
import jax
import jax.numpy as jnp
from jax import lax
from jax.sharding import PartitionSpec as P

MAXM = 64
eps = 1e-06


def passed_along(block, axis, distance):
    devices = range(lax.axis_size(axis))
    route = [(i - distance, i) for i in devices if i - distance in devices]
    return lax.ppermute(block, axis, route)


def correlate(window, batches):
    batch_count, tmpl_count, local_sta, comp_count, span_len = batches.shape
    kernels = jnp.transpose(batches, (2, 0, 1, 3, 4)).reshape(
        local_sta * batch_count * tmpl_count, comp_count, span_len
    )
    records = window.reshape(1, local_sta * comp_count, window.shape[2])
    products = lax.conv_general_dilated(
        records,
        kernels,
        (1,),
        "VALID",
        dimension_numbers=("NCH", "OIH", "NCH"),
        feature_group_count=local_sta,
        preferred_element_type=jnp.float32,
    )
    products = products.reshape(local_sta, batch_count * tmpl_count, products.shape[2])
    squares = jnp.sum(jnp.square(window.astype(jnp.float32)), axis=1)
    energy = lax.reduce_window(squares, 0.0, lax.add, (1, span_len), (1, 1), "VALID") / (
        comp_count * span_len
    )
    tmpl_power = jnp.sum(jnp.square(batches.astype(jnp.float32)), axis=(3, 4)) / (
        comp_count * span_len
    )
    tmpl_power = jnp.transpose(tmpl_power, (2, 0, 1)).reshape(local_sta, batch_count * tmpl_count)
    return products / (
        comp_count
        * span_len
        * jnp.sqrt(tmpl_power + eps)[:, :, None]
        * jnp.sqrt(energy + eps)[None, :, :].transpose(1, 0, 2)
    )


def shift_rows(scores, lag_table, stretch_len):

    def one_row(row, lag_value):
        return lax.dynamic_slice_in_dim(row, lag_value, stretch_len, 0)

    return jax.vmap(jax.vmap(one_row))(scores, lag_table)


def shards(data, bank, owners, moveouts):
    local_sta, comp_count, stretch_len = data.shape
    span_len = bank.shape[-1]
    tmpl_count = bank.shape[1]
    batch_count = owners.shape[0]
    owned_bank = bank[0]
    device_pos = lax.axis_index("tm")
    masked = jnp.stack(
        [
            jnp.where(owners[batch_id] == device_pos, owned_bank.astype(jnp.float32), 0.0)
            for batch_id in range(batch_count)
        ]
    )
    batches = lax.psum(masked, "tm").astype(jnp.bfloat16)
    edge_cells = passed_along(data[:, :, : span_len - 1 + MAXM], "tm", -1)
    scores = correlate(jnp.concatenate([data, edge_cells], axis=2), batches)
    lag_table = jnp.transpose(moveouts, (2, 0, 1)).reshape(local_sta, batch_count * tmpl_count)
    shifted = shift_rows(scores, lag_table, stretch_len)
    partial_sum = jnp.sum(shifted, axis=0).reshape(batch_count, tmpl_count, stretch_len)
    return lax.psum_scatter(partial_sum, "sta", scatter_dimension=1, tiled=True)


def solution(mesh):
    placed = (P("sta", None, "tm"), P("tm", None, "sta", None, None), P(), P(None, None, "sta"))
    return jax.shard_map(
        shards, mesh=mesh, in_specs=placed, out_specs=P(None, "sta", "tm"), check_vma=False
    )
```

profile of v0, /device:TPU:2, one launch (start us, length us, event | category | flops | bytes accessed | tf_op | source)
XLA Modules:
  0.0 800.6 jit_solution(17727927830055742186)
XLA Ops:
  6.4 277.5 %all-reduce.2 = bf16[2,8,8,3,150]{4,1,0,3,2:T(8,128)(2,1)S(1)} all-reduce(f32[2,8,8,3,150]{4,1,0,3,2:T(8,128)S(1)} %pad_maximum_fusion), channel_id=1, replica_groups=mesh['tm'=64,'sta'=8] {'tm'}, use_global_device_ids=true, to_apply=%region_0.1 | all-reduce | flops 57600 | bytes 345600 | tf_op jit(solution)/shard_map/psum | solution.py:69
  284.3 2.0 copy.43
  288.9 2.5 copy.42
  291.4 9.1 %reduce_window_sum.9 = f32[8,448]{1,0:T(8,128)S(1)} reduce-window(f32[8,597]{1,0:T(8,128)S(1)} %multiply_reduce_fusion.1, f32[]{:T(128)} %constant.6.clone.1), window={size=1x150}, to_apply=%region_3.4 | reduce-window | flops 534016 | bytes 33444 | tf_op jit(solution)/shard_map/reduce_window_sum | solution.py:33
  301.4 98.9 %fusion.2 = f32[1,8,16,448]{2,0,1,3:T(1,128)S(1)} fusion(bf16[1,8,3,597]{2,0,1,3:T(2,128)(2,1)S(1)} %copy.42, bf16[8,16,3,150]{1,2,0,3:T(4,128)(2,1)} %copy.43), kind=kOutput, calls=%fused_computation.18 | convolution fusion | flops 51609600 | bytes 373232 | tf_op jit(solution)/shard_map/conv_general_dilated | solution.py:22
  401.8 344.8 %while.1 = (s32[]{:T(128)}, f32[8,16,448]{2,1,0:T(8,128)S(1)}, s32[128,3]{0,1:T(4,128)S(1)}, f32[128,384]{1,0:T(8,128)S(1)}, s32[]{:T(128)}, /*index=5*/s32[]{:T(128)}) while((s32[]{:T(128)}, f32[8,16,448]{2,1,0:T(8,128)S(1)}, s32[128,3]{0,1:T(4,128)S(1)}, f32[128,384]{1,0:T(8,128)S(1)}, s32[]{:T(128)}, /*index=5*/s32[]{:T(128)}) %tuple.32), condition=%wide.while_cond, body=%wide.while_body.sunk | while | flops 2 | bytes 6281 | solution.py:51
  402.5 2.0 dynamic-slice_bitcast_fusion.2
  407.9 2.0 dynamic-slice_bitcast_fusion.2
  410.6 2.0 dynamic-slice_bitcast_fusion.2
  416.0 2.0 dynamic-slice_bitcast_fusion.2
  421.3 2.0 dynamic-slice_bitcast_fusion.2
  426.7 2.0 dynamic-slice_bitcast_fusion.2
  432.1 2.0 dynamic-slice_bitcast_fusion.2
  437.5 2.0 dynamic-slice_bitcast_fusion.2
  442.9 2.0 dynamic-slice_bitcast_fusion.2
  448.3 2.0 dynamic-slice_bitcast_fusion.2
  453.7 2.0 dynamic-slice_bitcast_fusion.2
  459.1 2.0 dynamic-slice_bitcast_fusion.2
  461.8 2.0 dynamic-slice_bitcast_fusion.2
  467.1 2.0 dynamic-slice_bitcast_fusion.2
  472.5 2.0 dynamic-slice_bitcast_fusion.2
  477.9 2.0 dynamic-slice_bitcast_fusion.2
  483.3 2.0 dynamic-slice_bitcast_fusion.2
  746.7 52.7 %all-reduce = f32[2,8,384]{2,0,1:T(2,128)S(1)} all-reduce(f32[2,8,384]{2,0,1:T(2,128)S(1)} %copy.49), channel_id=2, replica_groups=mesh['tm'=64,'sta'=8] {'sta'}, use_global_device_ids=true, to_apply=%region_5.6.clone | all-reduce | flops 6144 | bytes 49152
  (534 shorter events, 320.0 us)
Async XLA Ops:
  0.0 284.2 %copy-start.4 = (s32[2,8,8]{2,1,0:T(8,128)S(1)}, s32[2,8,8]{2,1,0:T(8,128)}, u32[]{:S(2)}) copy-start(s32[2,8,8]{2,1,0:T(8,128)} %param.7) | copy-start | bytes 1540
  0.7 288.2 %collective-permute-start = (bf16[8,3,213]{2,0,1:T(8,128)(2,1)S(1)}, bf16[8,3,213]{2,0,1:T(8,128)(2,1)S(1)}, u32[]{:S(2)}, u32[]{:S(2)}) collective-permute-start(bf16[8,3,213]{2,0,1:T(8,128)(2,1)S(1)} %slice.9), channel_id=1, source_target_pairs={{8,0},{16,8},{24,16},{32,24},{40,32},{48,40},{56,48},{64,56},{72,6... | collective-permute-start | bytes 30680 | tf_op jit(solution)/shard_map/ppermute | solution.py:13
  301.4 98.9 %copy-start = (f32[8,448]{0,1:T(8,128)S(1)}, f32[8,448]{0,1:T(8,128)}, u32[]{:S(2)}) copy-start(f32[8,448]{0,1:T(8,128)} %copy.46) | copy-start | bytes 43012
  301.4 98.9 %copy-start.3 = (f32[8,16]{1,0:T(8,128)S(1)}, f32[8,16]{1,0:T(8,128)}, u32[]{:S(2)}) copy-start(f32[8,16]{1,0:T(8,128)} %copy.51) | copy-start | bytes 1540
  400.9 0.9 copy-start.1
  400.9 0.9 copy-start.2
where the time goes:
time: 804 us; the launch traced here: 801 us
  local copies, waits for them, and re-layouts  355 us (44%)
  blocking collectives  330 us (41%)
  matrix products  98.9 us (12%)
  other arithmetic  10.8 us (1%)
    gather x512, local copies, waits for them, and re-layouts  342 us
    psum x1, blocking collectives, shards(): batches = lax.psum(masked, 'tm').astype(jnp.bfloat16)  278 us
    conv_general_dilated x1, matrix products, correlate(): lax.conv_general_dilated(records, kernels, (1,), 'VALID', dimension_numbe...  98.9 us
    unnamed x1, blocking collectives  52.7 us
  transfers between devices with their start and end apart: 1, of which 0 were waited for; matrix products, arithmetic and copies ran while one was open for 1% of the time, Pallas kernels for 0%

commit v1 on v0

--- a/solution.py
+++ b/solution.py
@@ -66,7 +66,7 @@
             for batch_id in range(batch_count)
         ]
     )
-    batches = lax.psum(masked, "tm").astype(jnp.bfloat16)
+    batches = jnp.sum(lax.all_gather(masked, "tm"), axis=0).astype(jnp.bfloat16)
     edge_cells = passed_along(data[:, :, : span_len - 1 + MAXM], "tm", -1)
     scores = correlate(jnp.concatenate([data, edge_cells], axis=2), batches)
     lag_table = jnp.transpose(moveouts, (2, 0, 1)).reshape(local_sta, batch_count * tmpl_count)

time: 804 us -> 691 us (0.86)
  the two profiles are of different devices: /device:TPU:2 before, /device:TPU:8 now
where the time goes in v1:
time: 691 us; the launch traced here: 688 us
  local copies, waits for them, and re-layouts  357 us (52%)
  waiting for transfers between devices  131 us (19%)
  matrix products  98.9 us (14%)
  blocking collectives  54.6 us (8%)
  other arithmetic  21 us (3%)
  between operations  14.9 us (2%)
  starting transfers between devices  7.21 us (1%)
    gather x512, local copies, waits for them, and re-layouts  342 us
    all_gather x1, waiting for transfers between devices, shards(): batches = jnp.sum(lax.all_gather(masked, 'tm'), axis=0).astype(jnp.bfloat16)  131 us
    conv_general_dilated x1, matrix products, correlate(): lax.conv_general_dilated(records, kernels, (1,), 'VALID', dimension_numbe...  98.9 us
    unnamed x1, blocking collectives  54.6 us
  transfers between devices with their start and end apart: 2, of which 1 were waited for; matrix products, arithmetic and copies ran while one was open for 2% of the time, Pallas kernels for 0%

profile of v1, /device:TPU:8, one launch (start us, length us, event | category | flops | bytes accessed | tf_op | source)
XLA Modules:
  0.0 687.5 jit_solution(14592448463182757943)
XLA Ops:
  11.8 7.2 %collective-permute-start = (bf16[8,3,213]{2,0,1:T(8,128)(2,1)S(1)}, bf16[8,3,213]{2,0,1:T(8,128)(2,1)S(1)}, u32[]{:S(2)}, u32[]{:S(2)}) collective-permute-start(bf16[8,3,213]{2,0,1:T(8,128)(2,1)S(1)} %slice.9), channel_id=1, source_target_pairs={{8,0},{16,8},{24,16},{32,24},{40,32},{48,40},{56,48},{64,56},{72,6... | collective-permute-start | bytes 30680 | tf_op jit(solution)/shard_map/ppermute | solution.py:13
  22.4 2.5 copy.31
  24.9 9.1 %reduce_window_sum.9 = f32[8,448]{1,0:T(8,128)S(1)} reduce-window(f32[8,597]{1,0:T(8,128)S(1)} %multiply_reduce_fusion.1, f32[]{:T(128)} %constant.6.clone.1), window={size=1x150}, to_apply=%region_3.4 | reduce-window | flops 534016 | bytes 33444 | tf_op jit(solution)/shard_map/reduce_window_sum | solution.py:33
  34.9 130.9 %all-gather.3.cloned.1.call-done = f32[128,8,8,3,150]{4,2,3,1,0:T(8,128)} async-done(((f32[2,8,8,3,150]{4,2,3,1,0:T(8,128)}), f32[128,8,8,3,150]{4,2,3,1,0:T(8,128)}) %all-gather.3.cloned.1.call-update) | async-done | bytes 14745616 | tf_op jit(solution)/shard_map/all_gather | solution.py:69
  165.8 9.4 %reduce_sum.36 = bf16[2,8,8,3,150]{4,2,3,1,0:T(8,128)(2,1)S(1)} reduce(f32[64,2,8,8,3,150]{5,3,4,2,1,0:T(8,128)} %bitcast.35, f32[]{:T(128)} %constant.6.clone.1), dimensions={0}, to_apply=%region_0.1 | reduce | flops 3628800 | bytes 14860804 | tf_op jit(solution)/shard_map/reduce_sum | solution.py:69
  175.3 3.6 copy.32
  179.6 98.9 %fusion.2 = f32[1,8,16,448]{2,0,1,3:T(1,128)S(1)} fusion(bf16[1,8,3,597]{2,0,1,3:T(2,128)(2,1)S(1)} %copy.31, bf16[8,16,3,150]{1,2,0,3:T(4,128)(2,1)} %copy.32), kind=kOutput, calls=%fused_computation.17 | convolution fusion | flops 51609600 | bytes 373232 | tf_op jit(solution)/shard_map/conv_general_dilated | solution.py:22
  280.0 344.8 %while.1 = (s32[]{:T(128)}, f32[8,16,448]{2,1,0:T(8,128)S(1)}, s32[128,3]{0,1:T(4,128)S(1)}, f32[128,384]{1,0:T(8,128)S(1)}, s32[]{:T(128)}, /*index=5*/s32[]{:T(128)}) while((s32[]{:T(128)}, f32[8,16,448]{2,1,0:T(8,128)S(1)}, s32[128,3]{0,1:T(4,128)S(1)}, f32[128,384]{1,0:T(8,128)S(1)}, s32[]{:T(128)}, /*index=5*/s32[]{:T(128)}) %tuple.33), condition=%wide.while_cond, body=%wide.while_body.sunk | while | flops 2 | bytes 6281 | solution.py:51
  283.4 2.0 dynamic-slice_bitcast_fusion.2
  288.8 2.0 dynamic-slice_bitcast_fusion.2
  294.2 2.0 dynamic-slice_bitcast_fusion.2
  296.9 2.0 dynamic-slice_bitcast_fusion.2
  302.3 2.0 dynamic-slice_bitcast_fusion.2
  307.7 2.0 dynamic-slice_bitcast_fusion.2
  313.0 2.0 dynamic-slice_bitcast_fusion.2
  318.4 2.0 dynamic-slice_bitcast_fusion.2
  323.8 2.0 dynamic-slice_bitcast_fusion.2
  329.2 2.0 dynamic-slice_bitcast_fusion.2
  334.6 2.0 dynamic-slice_bitcast_fusion.2
  340.0 2.0 dynamic-slice_bitcast_fusion.2
  345.4 2.0 dynamic-slice_bitcast_fusion.2
  348.1 2.0 dynamic-slice_bitcast_fusion.2
  353.5 2.0 dynamic-slice_bitcast_fusion.2
  624.9 54.6 %all-reduce = f32[2,8,384]{2,0,1:T(2,128)S(1)} all-reduce(f32[2,8,384]{2,0,1:T(2,128)S(1)} %copy.37), channel_id=3, replica_groups=mesh['tm'=64,'sta'=8] {'sta'}, use_global_device_ids=true, to_apply=%region_5.6.clone | all-reduce | flops 6144 | bytes 49152
  (534 shorter events, 324.0 us)
Async XLA Ops:
  6.5 159.2 %all-gather.3.cloned.1.call-start = ((), (), s32[]{:S(2)}) async-start(), calls=%async_computation | async-start | bytes 25559040 | tf_op jit(solution)/shard_map/all_gather | solution.py:69
  11.8 10.7 %collective-permute-start = (bf16[8,3,213]{2,0,1:T(8,128)(2,1)S(1)}, bf16[8,3,213]{2,0,1:T(8,128)(2,1)S(1)}, u32[]{:S(2)}, u32[]{:S(2)}) collective-permute-start(bf16[8,3,213]{2,0,1:T(8,128)(2,1)S(1)} %slice.9), channel_id=1, source_target_pairs={{8,0},{16,8},{24,16},{32,24},{40,32},{48,40},{56,48},{64,56},{72,6... | collective-permute-start | bytes 30680 | tf_op jit(solution)/shard_map/ppermute | solution.py:13
  179.6 98.9 %copy-start = (f32[8,448]{0,1:T(8,128)S(1)}, f32[8,448]{0,1:T(8,128)}, u32[]{:S(2)}) copy-start(f32[8,448]{0,1:T(8,128)} %copy.34) | copy-start | bytes 43012
  179.6 98.9 %copy-start.3 = (f32[8,16]{1,0:T(8,128)S(1)}, f32[8,16]{1,0:T(8,128)}, u32[]{:S(2)}) copy-start(f32[8,16]{1,0:T(8,128)} %copy.41) | copy-start | bytes 1540
  279.1 0.9 copy-start.1
  279.1 0.9 copy-start.2
Sparse Core Ops, SparseCore 0:
  11.2 154.5 all-gather.2
